TPU v7x, 256 devices: a whole 4x4x8 slice. The times are simulated.
256 devices in a mesh: row: 16 (over x, z_lo, core), col: 16 (over y, z_hi).
Axes of the slice: x: 4, y: 4, z: 8 (z_hi: 4, z_lo: 2; z = z_hi * 2 + z_lo), core: 2. Of those that a mesh axis runs over, the one named last changes fastest.
Arguments:
- vectors: bfloat16 [2048, 1024], P(('row', 'col')), may hold values from -6 to 6
- block_values: bfloat16 [16, 16, 512, 4096], P('row', 'col'), may hold values from -0.09375 to 0.09375
- block_rows: int32 [16, 16, 512], P('row', 'col'), may hold values from 0 to 127, as said below
- block_cols: int32 [16, 16, 512], P('row', 'col'), may hold values from 0 to 127, as said below
- block_count: int32 [16, 16], P('row', 'col'), may hold values from 0 to 512, as said below
Outputs:
- product: float32 [2048, 1024], P(('row', 'col'))
Inputs may be any that keep to these rules, and one draw needn't show every extreme that they name: `block_rows`: in each tile the live slots name distinct positions with gi >= gj and come first, sorted by block row and then block column; slots past the count hold in-range indices that are not part of the matrix. `block_cols`: same slots as block_rows. `block_count`: some tile fills all 512 slots in every draw.
All inputs are finite; a program needn't handle non-finite values.
Results may differ from a plain program's by a relative error of at most 0.0003.
Values may be sent and summed in bfloat16 or wider, within the bound.
No kernel may reach another device: no remote copies, remote signals or barrier semaphores. Data moves between devices by JAX's collectives and lax.ppermute only.
A program may use at most 64 MiB of HBM per device.

v0:
```python
import jax
import jax.numpy as jnp
from jax import lax
from jax.sharding import PartitionSpec as P

NV = 16
BS = 64


def on_device(vectors, block_values, block_rows, block_cols, block_count):
    col_devices = lax.axis_size("col")
    row_index = lax.axis_index("row")
    col_index = lax.axis_index("col")
    piece_blocks = vectors.shape[0]
    width = vectors.shape[1]
    slot_count = block_rows.shape[2]
    matrices = block_values.reshape(slot_count, BS, BS)
    local_rows = block_rows.reshape(slot_count)
    local_cols = block_cols.reshape(slot_count)
    live_count = block_count.reshape(())
    row_segment = lax.all_gather(vectors, "col", axis=0, tiled=True)
    column_set = lax.all_gather(vectors, "row", axis=0, tiled=True)
    global_row = row_index * col_devices * piece_blocks + local_rows
    global_col = (
        local_cols // piece_blocks * col_devices + col_index
    ) * piece_blocks + local_cols % piece_blocks
    live = jnp.arange(slot_count, dtype=jnp.int32) < live_count
    weight = jnp.where(live, jnp.where(global_row == global_col, 0.5, 1.0), 0.0).astype(jnp.float32)
    col_vectors = jnp.take(column_set, local_cols, axis=0).reshape(slot_count, NV, BS)
    row_vectors = jnp.take(row_segment, local_rows, axis=0).reshape(slot_count, NV, BS)
    forward = jnp.einsum("nvk,nik->nvi", col_vectors, matrices, preferred_element_type=jnp.float32)
    backward = jnp.einsum("nvi,nik->nvk", row_vectors, matrices, preferred_element_type=jnp.float32)
    forward = (forward * weight[:, None, None]).reshape(slot_count, width)
    backward = (backward * weight[:, None, None]).reshape(slot_count, width)
    row_part = jax.ops.segment_sum(forward, local_rows, num_segments=row_segment.shape[0])
    col_part = jax.ops.segment_sum(backward, local_cols, num_segments=column_set.shape[0])
    whole_rows = lax.psum(row_part, "col")
    whole_cols = lax.psum(col_part, "row")
    mine_rows = lax.dynamic_slice_in_dim(whole_rows, col_index * piece_blocks, piece_blocks, 0)
    mine_cols = lax.dynamic_slice_in_dim(whole_cols, row_index * piece_blocks, piece_blocks, 0)
    return mine_rows + mine_cols


def solution(mesh):
    placed = (
        P(("row", "col"), None),
        P("row", "col", None, None),
        P("row", "col", None),
        P("row", "col", None),
        P("row", "col"),
    )
    return jax.shard_map(
        on_device, mesh=mesh, in_specs=placed, out_specs=P(("row", "col"), None), check_vma=False
    )
```

profile of v0, /device:TPU:1, one launch (start us, length us, event | category | flops | bytes accessed | tf_op | source)
XLA Modules:
  0.0 377.8 jit_solution(11786903282523296864)
XLA Ops:
  6.5 0.0 all-reduce.3.cloned.1.call-start
  6.5 0.7 add_select_fusion
  7.2 0.7 compare_and_fusion.1
  8.6 22.6 %all_gather.6 = bf16[128,1024]{1,0:T(8,128)(2,1)S(1)} all-gather(bf16[8,1024]{1,0:T(8,128)(2,1)} %param.7), channel_id=1, replica_groups=mesh['row'=16,'col'=16] {'row'}, dimensions={0}, use_global_device_ids=true | all-gather | bytes 278528 | tf_op jit(solution)/shard_map/all_gather | solution.py:22
  31.2 2.1 gather_fusion
  33.3 1.2 broadcast_select_fusion.1
  34.4 1.5 copy.6
  35.9 2.0 copy.8
  38.0 6.5 %copy.7 = bf16[1,1,512,4096]{2,3,1,0:T(8,128)(2,1)} copy(bf16[1,1,512,4096]{3,2,1,0:T(8,128)(2,1)} %param.8) | data formatting | bytes 8388608 | tf_op args[1]
  44.5 13.0 %copy.9 = bf16[512,64,64]{2,1,0:T(8,128)(2,1)} copy(bf16[512,64,64]{0,2,1:T(8,128)(2,1)} %bitcast.13) | data formatting | bytes 8388608 | tf_op jit(solution)/shard_map/reshape | solution.py:17
  57.5 0.0 copy-done.1
  57.5 9.8 %convolution_multiply_fusion.1 = f32[512,16,64]{2,1,0:T(8,128)} fusion(bf16[512,16,64]{2,1,0:T(8,128)(2,1)S(1)} %copy.8, bf16[512,64,64]{2,1,0:T(8,128)(2,1)} %copy.9, f32[512]{0:T(512)S(1)} %select_select_fusion), kind=kOutput, calls=%fused_computation.5 | convolution fusion | flops 67633152 | bytes 7342080 | tf_op jit(solution)/shard_map/nvk,nik->nvi/dot_general | solution.py:31
  67.3 2.8 copy.10
  70.1 0.0 copy-start
  70.2 1.9 copy.11
  72.0 6.5 %scatter_custom_fusion = f32[128,1024]{1,0:T(8,128)} fusion(s32[512]{0:T(512)S(1)} %bitcast.19, f32[512,1024]{1,0:T(8,128)} %copy.11, f32[]{:T(128)} %constant.47.clone.1), kind=kCustom, calls=%fused_computation.10 | custom fusion | flops 524288 | bytes 524800 | tf_op jit(solution)/shard_map/scatter-add | solution.py:35
  78.6 0.0 all-reduce.3.cloned.1.call-update
  78.6 0.0 all-reduce.5.cloned.1.call-start
  78.6 0.0 copy-done
  78.7 41.2 %all_gather.7 = bf16[128,1024]{1,0:T(8,128)(2,1)S(1)} all-gather(bf16[8,1024]{1,0:T(8,128)(2,1)S(1)} %copy-done), channel_id=1, replica_groups=mesh['row'=16,'col'=16] {'col'}, dimensions={0}, use_global_device_ids=true | all-gather | bytes 278528 | tf_op jit(solution)/shard_map/all_gather | solution.py:21
  119.8 2.1 gather_fusion.1
  121.9 1.2 broadcast_select_fusion
  123.1 1.5 copy.12
  124.6 2.0 copy.13
  126.7 7.7 %convolution_multiply_fusion = f32[512,16,64]{2,1,0:T(8,128)} fusion(bf16[512,16,64]{2,1,0:T(8,128)(2,1)S(1)} %copy.13, bf16[512,64,64]{2,1,0:T(8,128)(2,1)} %copy.9, f32[512]{0:T(512)S(1)} %select_select_fusion), kind=kOutput, calls=%fused_computation.4 | convolution fusion | flops 67633152 | bytes 7342080 | tf_op jit(solution)/shard_map/nvi,nik->nvk/dot_general | solution.py:32
  134.4 2.8 copy.15
  137.2 1.9 copy.16
  139.1 6.5 %scatter_custom_fusion.1 = f32[128,1024]{1,0:T(8,128)} fusion(s32[512]{0:T(512)S(1)} %bitcast.25, f32[512,1024]{1,0:T(8,128)} %copy.16, f32[]{:T(128)} %constant.47.clone.1), kind=kCustom, calls=%fused_computation.8 | custom fusion | flops 524288 | bytes 524800 | tf_op jit(solution)/shard_map/scatter-add | solution.py:36
  145.6 0.0 all-reduce.5.cloned.1.call-update
  145.6 89.8 %all-reduce.3.cloned.1.call-done = f32[128,1024]{1,0:T(8,128)} async-done(((f32[128,1024]{1,0:T(8,128)}), f32[128,1024]{1,0:T(8,128)}) %all-reduce.3.cloned.1.call-update) | async-done | bytes 524304 | tf_op jit(solution)/shard_map/psum | solution.py:37
  235.3 134.3 %all-reduce.5.cloned.1.call-done = f32[128,1024]{1,0:T(8,128)} async-done(((f32[128,1024]{1,0:T(8,128)}), f32[128,1024]{1,0:T(8,128)}) %all-reduce.5.cloned.1.call-update) | async-done | bytes 524304 | tf_op jit(solution)/shard_map/psum | solution.py:38
  369.6 1.4 dynamic-slice_add_fusion
  (8 shorter events, 0.0 us)
Async XLA Ops:
  6.5 228.8 %all-reduce.3.cloned.1.call-start = ((), (), s32[]{:S(2)}) async-start(), calls=%async_computation | async-start | bytes 1048576 | tf_op jit(solution)/shard_map/psum | solution.py:37
  44.5 13.0 %copy-start.1 = (s32[1,1,512]{2,1,0:T(1,128)S(1)}, s32[1,1,512]{2,1,0:T(1,128)}, u32[]{:S(2)}) copy-start(s32[1,1,512]{2,1,0:T(1,128)} %param.9) | copy-start | bytes 6148
  44.5 13.0 %copy-start.2 = (s32[1,1,512]{2,1,0:T(1,128)S(1)}, s32[1,1,512]{2,1,0:T(1,128)}, u32[]{:S(2)}) copy-start(s32[1,1,512]{2,1,0:T(1,128)} %param.10) | copy-start | bytes 6148
  70.1 8.5 %copy-start = (bf16[8,1024]{1,0:T(8,128)(2,1)S(1)}, bf16[8,1024]{1,0:T(8,128)(2,1)}, u32[]{:S(2)}) copy-start(bf16[8,1024]{1,0:T(8,128)(2,1)} %param.7) | copy-start | bytes 49156
  78.6 291.0 %all-reduce.5.cloned.1.call-start = ((), (), s32[]{:S(2)}) async-start(), calls=%async_computation.1 | async-start | bytes 1048576 | tf_op jit(solution)/shard_map/psum | solution.py:38
Sparse Core Ops, SparseCore 0:
  78.7 156.5 all-reduce.2
  237.9 131.6 all-reduce.4
where the time goes:
time: 379 us; the launch traced here: 378 us
  waiting for transfers between devices  224 us (59%)
  blocking collectives  63.8 us (17%)
  local copies, waits for them, and re-layouts  40.1 us (11%)
  other arithmetic  18.2 us (5%)
  matrix products  17.5 us (5%)
  between operations  14.2 us (4%)
    psum x1, waiting for transfers between devices, on_device(): whole_cols = lax.psum(col_part, 'row')  134 us
    psum x1, waiting for transfers between devices, on_device(): whole_rows = lax.psum(row_part, 'col')  89.8 us
    all_gather x1, blocking collectives, on_device(): row_segment = lax.all_gather(vectors, 'col', axis=0, tiled=True)  41.2 us
    all_gather x1, blocking collectives, on_device(): column_set = lax.all_gather(vectors, 'row', axis=0, tiled=True)  22.6 us
    reshape x1, local copies, waits for them, and re-layouts, on_device(): matrices = block_values.reshape(slot_count, BS, BS)  13 us
    dot_general x1, matrix products, on_device(): jnp.einsum('nvk,nik->nvi', col_vectors, matrices, preferred_element_type=...  9.8 us
    dot_general x1, matrix products, on_device(): jnp.einsum('nvi,nik->nvk', row_vectors, matrices, preferred_element_type=...  7.68 us
  transfers between devices with their start and end apart: 2, of which 2 were waited for; matrix products, arithmetic and copies ran while one was open for 7% of the time, Pallas kernels for 0%

commit v1 on v0

--- a/solution.py
+++ b/solution.py
@@ -35,7 +35,7 @@
     row_part = jax.ops.segment_sum(forward, local_rows, num_segments=row_segment.shape[0])
     col_part = jax.ops.segment_sum(backward, local_cols, num_segments=column_set.shape[0])
     whole_rows = lax.psum(row_part, "col")
-    whole_cols = lax.psum(col_part, "row")
+    whole_cols = jnp.sum(lax.all_gather(col_part, "row"), axis=0)
     mine_rows = lax.dynamic_slice_in_dim(whole_rows, col_index * piece_blocks, piece_blocks, 0)
     mine_cols = lax.dynamic_slice_in_dim(whole_cols, row_index * piece_blocks, piece_blocks, 0)
     return mine_rows + mine_cols

time: 379 us -> 322 us (0.85)
  the two profiles are of different devices: /device:TPU:1 before, /device:TPU:2 now
where the time goes in v1:
time: 322 us
  waiting for transfers between devices  158 us (49%)
  blocking collectives  67.8 us (21%)
  local copies, waits for them, and re-layouts  40.1 us (12%)
  other arithmetic  22.4 us (7%)
  matrix products  17.5 us (5%)
  between operations  15.6 us (5%)
    psum x1, waiting for transfers between devices, on_device(): whole_rows = lax.psum(row_part, 'col')  157 us
    all_gather x1, blocking collectives, on_device(): row_segment = lax.all_gather(vectors, 'col', axis=0, tiled=True)  48.4 us
    all_gather x1, blocking collectives, on_device(): column_set = lax.all_gather(vectors, 'row', axis=0, tiled=True)  19.4 us
    reshape x1, local copies, waits for them, and re-layouts, on_device(): matrices = block_values.reshape(slot_count, BS, BS)  13 us
    dot_general x1, matrix products, on_device(): jnp.einsum('nvk,nik->nvi', col_vectors, matrices, preferred_element_type=...  9.91 us
    dot_general x1, matrix products, on_device(): jnp.einsum('nvi,nik->nvk', row_vectors, matrices, preferred_element_type=...  7.62 us
    scatter-add x1, other arithmetic, on_device(): jax.ops.segment_sum(forward, local_rows, num_segments=row_segment.shape[0])  6.58 us
    unnamed x7, local copies, waits for them, and re-layouts  6.49 us
  transfers between devices with their start and end apart: 2, of which 2 were waited for; matrix products, arithmetic and copies ran while one was open for 10% of the time, Pallas kernels for 0%

profile of v1, /device:TPU:2, one launch (start us, length us, event | category | flops | bytes accessed | tf_op | source)
XLA Modules:
  0.0 321.6 jit_solution(4255815016865871088)
XLA Ops:
  7.4 0.0 all-gather.3.cloned.1.call-start
  7.4 0.7 compare_select_fusion
  8.1 0.7 compare_and_fusion
  9.4 48.4 %all_gather.13 = bf16[128,1024]{1,0:T(8,128)(2,1)S(1)} all-gather(bf16[8,1024]{1,0:T(8,128)(2,1)} %param.7), channel_id=1, replica_groups=mesh['row'=16,'col'=16] {'col'}, dimensions={0}, use_global_device_ids=true | all-gather | bytes 278528 | tf_op jit(solution)/shard_map/all_gather | solution.py:21
  57.8 2.1 gather_fusion.1
  59.9 1.2 broadcast_select_fusion
  61.0 1.5 copy.12
  62.5 2.0 copy.13
  64.5 6.5 %copy.7 = bf16[1,1,512,4096]{2,3,1,0:T(8,128)(2,1)} copy(bf16[1,1,512,4096]{3,2,1,0:T(8,128)(2,1)} %param.8) | data formatting | bytes 8388608 | tf_op args[1]
  71.0 13.0 %copy.9 = bf16[512,64,64]{2,1,0:T(8,128)(2,1)} copy(bf16[512,64,64]{0,2,1:T(8,128)(2,1)} %bitcast.14) | data formatting | bytes 8388608 | tf_op jit(solution)/shard_map/reshape | solution.py:17
  84.0 7.6 %convolution_multiply_fusion = f32[512,16,64]{2,1,0:T(8,128)} fusion(bf16[512,16,64]{2,1,0:T(8,128)(2,1)S(1)} %copy.13, bf16[512,64,64]{2,1,0:T(8,128)(2,1)} %copy.9, f32[512]{0:T(512)S(1)} %select_select_fusion), kind=kOutput, calls=%fused_computation.4 | convolution fusion | flops 67633152 | bytes 7342080 | tf_op jit(solution)/shard_map/nvi,nik->nvk/dot_general | solution.py:32
  91.6 2.8 copy.15
  94.5 0.0 copy-start
  94.5 1.9 copy.16
  96.3 6.5 %scatter_custom_fusion.1 = f32[128,1024]{1,0:T(8,128)} fusion(s32[512]{0:T(512)S(1)} %bitcast.21, f32[512,1024]{1,0:T(8,128)} %copy.16, f32[]{:T(128)} %constant.47.clone.1), kind=kCustom, calls=%fused_computation.8 | custom fusion | flops 524288 | bytes 524800 | tf_op jit(solution)/shard_map/scatter-add | solution.py:36
  102.8 0.0 all-gather.3.cloned.1.call-update
  102.8 0.0 all-reduce.2.cloned.1.call-start
  102.9 0.0 copy-done
  102.9 19.4 %all_gather.12 = bf16[128,1024]{1,0:T(8,128)(2,1)S(1)} all-gather(bf16[8,1024]{1,0:T(8,128)(2,1)S(1)} %copy-done), channel_id=1, replica_groups=mesh['row'=16,'col'=16] {'row'}, dimensions={0}, use_global_device_ids=true | all-gather | bytes 278528 | tf_op jit(solution)/shard_map/all_gather | solution.py:22
  122.3 2.0 gather_fusion
  124.4 1.2 broadcast_select_fusion.1
  125.6 1.5 copy.6
  127.1 2.0 copy.8
  129.1 9.9 %convolution_multiply_fusion.1 = f32[512,16,64]{2,1,0:T(8,128)} fusion(bf16[512,16,64]{2,1,0:T(8,128)(2,1)S(1)} %copy.8, bf16[512,64,64]{2,1,0:T(8,128)(2,1)} %copy.9, f32[512]{0:T(512)S(1)} %select_select_fusion), kind=kOutput, calls=%fused_computation.5 | convolution fusion | flops 67633152 | bytes 7342080 | tf_op jit(solution)/shard_map/nvk,nik->nvi/dot_general | solution.py:31
  139.0 2.9 copy.10
  141.9 1.9 copy.11
  143.8 6.6 %scatter_custom_fusion = f32[128,1024]{1,0:T(8,128)} fusion(s32[512]{0:T(512)S(1)} %bitcast.27, f32[512,1024]{1,0:T(8,128)} %copy.11, f32[]{:T(128)} %constant.47.clone.1), kind=kCustom, calls=%fused_computation.10 | custom fusion | flops 524288 | bytes 524800 | tf_op jit(solution)/shard_map/scatter-add | solution.py:35
  150.4 0.0 all-reduce.2.cloned.1.call-update
  150.4 1.2 all-gather.3.cloned.1.call-done
  151.6 4.2 %reduce_sum.9 = f32[128,1024]{1,0:T(8,128)S(1)} reduce(f32[16,128,1024]{2,1,0:T(8,128)} %bitcast.17, f32[]{:T(128)} %constant.47.clone.1), dimensions={0}, to_apply=%region_3.5 | reduce | flops 1966080 | bytes 8912900 | tf_op jit(solution)/shard_map/reduce_sum | solution.py:38
  155.9 156.9 %all-reduce.2.cloned.1.call-done = f32[128,1024]{1,0:T(8,128)} async-done(((f32[128,1024]{1,0:T(8,128)}), f32[128,1024]{1,0:T(8,128)}) %all-reduce.2.cloned.1.call-update) | async-done | bytes 524304 | tf_op jit(solution)/shard_map/psum | solution.py:37
  312.7 1.4 dynamic-slice_add_fusion
  (9 shorter events, 0.0 us)
Async XLA Ops:
  7.4 144.3 %all-gather.3.cloned.1.call-start = ((), (), s32[]{:S(2)}) async-start(), calls=%async_computation.1 | async-start | bytes 8912896 | tf_op jit(solution)/shard_map/all_gather | solution.py:38
  71.0 13.0 %copy-start.1 = (s32[1,1,512]{2,1,0:T(1,128)S(1)}, s32[1,1,512]{2,1,0:T(1,128)}, u32[]{:S(2)}) copy-start(s32[1,1,512]{2,1,0:T(1,128)} %param.10) | copy-start | bytes 6148
  71.0 13.0 %copy-start.2 = (s32[1,1,512]{2,1,0:T(1,128)S(1)}, s32[1,1,512]{2,1,0:T(1,128)}, u32[]{:S(2)}) copy-start(s32[1,1,512]{2,1,0:T(1,128)} %param.9) | copy-start | bytes 6148
  94.5 8.5 %copy-start = (bf16[8,1024]{1,0:T(8,128)(2,1)S(1)}, bf16[8,1024]{1,0:T(8,128)(2,1)}, u32[]{:S(2)}) copy-start(bf16[8,1024]{1,0:T(8,128)(2,1)} %param.7) | copy-start | bytes 49156
  102.8 209.9 %all-reduce.2.cloned.1.call-start = ((), (), s32[]{:S(2)}) async-start(), calls=%async_computation | async-start | bytes 1048576 | tf_op jit(solution)/shard_map/psum | solution.py:37
Sparse Core Ops, SparseCore 0:
  103.0 48.6 all-gather.2
Sparse Core Ops, SparseCore 1:
  150.5 162.2 all-reduce.1
